TPU v7x, 128 devices: a whole 4x4x4 slice. The times are simulated.
128 devices in a mesh: req: 16 (over x, z), mlp: 8 (over y, core).
Axes of the slice: x: 4, y: 4, z: 4, core: 2. Of those that a mesh axis runs over, the one named last changes fastest.
Arguments:
- patches: bfloat16 [15360, 4096], P('req'), may hold values from -6 to 6
- norm_gain: float32 [4096], replicated, may hold values from 0.25 to 1.75
- norm_bias: float32 [4096], replicated, may hold values from -3 to 3
- gate_weight: bfloat16 [4096, 8192], P(None, ('req', 'mlp')), may hold values from -0.09375 to 0.09375
- up_weight: bfloat16 [4096, 8192], P(None, ('req', 'mlp')), may hold values from -0.09375 to 0.09375
- down_weight: bfloat16 [4096, 8192], P(None, ('req', 'mlp')), may hold values from -0.0625 to 0.0625
- layer_scale: float32 [4096], replicated, may hold values from 0.25 to 2.5
- projection: bfloat16 [4, 4096, 4096], P(None, 'mlp', 'req'), may hold values from -0.046875 to 0.046875
- text_rows: bfloat16 [65536, 4096], P(('req', 'mlp')), may hold values from -6 to 6
- destination: int32 [3840], replicated, may hold values from -1 to 65535, as said below
Outputs:
- patch_out: bfloat16 [15360, 4096], P('req', 'mlp')
- streams: bfloat16 [65536, 4096], P(('req', 'mlp'))
Inputs may be any that keep to these rules, and one draw needn't show every extreme that they name: `destination`: values other than -1 are distinct positions; the positions landing in one piece of 512 consecutive positions (a stream holds 8 pieces) form one run of consecutive positions, at least one and at most 30 of them, and some piece receives exactly 30.
All inputs are finite; a program needn't handle non-finite values.
Results may differ from a plain program's by a relative error of at most 0.015.
Values may be sent and summed in bfloat16 or wider, within the bound.
No kernel may reach another device: no remote copies, remote signals or barrier semaphores. Data moves between devices by JAX's collectives and lax.ppermute only.
A program may use at most 128 MiB of HBM per device.

v0:
```python
import jax
import jax.numpy as jnp
from jax import lax
from jax.sharding import PartitionSpec as P


def layer_norm(values, norm_gain, norm_bias):
    row_mean = jnp.mean(values, axis=-1, keepdims=True)
    centred = values - row_mean
    variance = jnp.mean(centred * centred, axis=-1, keepdims=True)
    return centred * lax.rsqrt(variance + 1e-06) * norm_gain + norm_bias


def shards(
    patches,
    norm_gain,
    norm_bias,
    gate_weight,
    up_weight,
    down_weight,
    layer_scale,
    projection,
    text_rows,
    destination,
):
    req_count = lax.axis_size("req")
    mlp_count = lax.axis_size("mlp")
    req_index = lax.axis_index("req")
    mlp_index = lax.axis_index("mlp")
    rows_here, model_width = patches.shape
    feat_width = model_width // mlp_count
    inputs = patches.astype(jnp.float32)
    normed = layer_norm(inputs, norm_gain, norm_bias).astype(jnp.bfloat16)
    gate_act = jnp.dot(
        normed,
        lax.all_gather(gate_weight, "req", axis=1, tiled=True),
        preferred_element_type=jnp.float32,
    )
    up_act = jnp.dot(
        normed,
        lax.all_gather(up_weight, "req", axis=1, tiled=True),
        preferred_element_type=jnp.float32,
    )
    hidden = (jax.nn.silu(gate_act) * up_act).astype(jnp.bfloat16)
    ffn_local = lax.dot_general(
        hidden,
        lax.all_gather(down_weight, "req", axis=1, tiled=True),
        (((1,), (1,)), ((), ())),
        preferred_element_type=jnp.float32,
    )
    partial_value = lax.optimization_barrier(ffn_local.astype(jnp.bfloat16)).astype(jnp.float32)
    ffn_feats = lax.psum_scatter(
        partial_value.astype(jnp.bfloat16), "mlp", scatter_dimension=1, tiled=True
    ).astype(jnp.float32)
    scale_here = lax.dynamic_slice_in_dim(layer_scale, mlp_index * feat_width, feat_width)
    own_inputs = lax.dynamic_slice_in_dim(inputs, mlp_index * feat_width, feat_width, axis=1)
    patch_out = (own_inputs + scale_here * ffn_feats).astype(jnp.bfloat16)
    merged = patch_out.reshape(rows_here // 4, 4 * feat_width)
    weight_cols = projection.reshape(4 * feat_width, projection.shape[2])
    piece_rows = text_rows.shape[0]
    slot_count = destination.shape[0]
    bucket_count = req_count * mlp_count
    capacity = slot_count // bucket_count
    is_valid = destination >= 0
    piece_ids = jnp.where(is_valid, destination // piece_rows, -1)
    offsets = destination % piece_rows
    bucket_hit = piece_ids[:, None] == jnp.arange(bucket_count, dtype=jnp.int32)[None, :]
    first_off = jnp.min(jnp.where(bucket_hit, offsets[:, None], piece_rows), axis=0)
    counts = jnp.sum(bucket_hit.astype(jnp.int32), axis=0)
    slot_first = jnp.sum(jnp.where(bucket_hit, first_off[None, :], 0), axis=1)
    slot_rank = offsets - slot_first
    stream_ids = piece_ids // mlp_count
    piece_in = piece_ids % mlp_count
    rows_at = piece_in * (req_count * capacity) + stream_ids * capacity + slot_rank
    rows_at = jnp.where(is_valid, rows_at, bucket_count * capacity)
    sources = (
        jnp.full((bucket_count * capacity,), -1, jnp.int32)
        .at[rows_at]
        .set(jnp.arange(slot_count, dtype=jnp.int32), mode="drop")
    )
    every_row = lax.all_gather(merged, "req", axis=0, tiled=True)
    picked_rows = jnp.take(every_row, jnp.maximum(sources, 0), axis=0)
    picked_rows = jnp.where(sources[:, None] >= 0, picked_rows, jnp.zeros_like(picked_rows))
    summed = lax.psum_scatter(
        jnp.dot(picked_rows, weight_cols, preferred_element_type=jnp.float32).astype(jnp.bfloat16),
        "mlp",
        scatter_dimension=0,
        tiled=True,
    )
    arrived = lax.all_to_all(summed, "req", split_axis=0, concat_axis=1, tiled=True)
    bucket_here = req_index * mlp_count + mlp_index
    start_here = first_off[bucket_here]
    count_here = counts[bucket_here]
    positions = jnp.arange(piece_rows, dtype=jnp.int32) - start_here
    inside = (positions >= 0) & (positions < count_here)
    image_rows = jnp.take(arrived, jnp.clip(positions, 0, capacity - 1), axis=0)
    streams = jnp.where(inside[:, None], image_rows, text_rows)
    return (patch_out, streams)


def solution(mesh):
    return jax.shard_map(
        shards,
        mesh=mesh,
        in_specs=(
            P("req", None),
            P(),
            P(),
            P(None, ("req", "mlp")),
            P(None, ("req", "mlp")),
            P(None, ("req", "mlp")),
            P(),
            P(None, "mlp", "req"),
            P(("req", "mlp"), None),
            P(),
        ),
        out_specs=(P("req", "mlp"), P(("req", "mlp"), None)),
        check_vma=False,
    )
```

profile of v0, /device:TPU:0, one launch (start us, length us, event | category | flops | bytes accessed | tf_op | source)
XLA Modules:
  0.0 527.9 jit_solution(9855831558795438825)
XLA Ops:
  7.2 0.7 all-gather.5.cloned.1.call-update
  8.0 0.7 all-gather.7.cloned.1.call-update
  8.7 0.7 all-gather.9.cloned.1.call-update
  9.5 4.5 convert_reduce_fusion
  14.0 1.0 copy-done.1
  14.9 2.2 multiply_reduce_fusion
  17.1 66.4 %all-gather.5.cloned.1.call-done = bf16[4096,1024]{0,1:T(8,128)(2,1)} async-done(((bf16[4096,64]{0,1:T(8,128)(2,1)}), bf16[4096,1024]{0,1:T(8,128)(2,1)}) %all-gather.5.cloned.1.call-update) | async-done | bytes 8388624 | tf_op jit(solution)/shard_map/all_gather | solution.py:36
  83.5 14.4 %fusion.31 = f32[960,1024]{1,0:T(8,128)} fusion(bf16[4096,1024]{0,1:T(8,128)(2,1)} %all-gather.5.cloned.1.call-done, bf16[960,4096]{1,0:T(8,128)(2,1)} %param.10, f32[4096]{0:T(1024)S(1)} %copy-done.4, f32[4096]{0:T(1024)S(1)} %copy-done.5, f32[960]{0:T(1024)S(1)} %add_rsqrt_fusion, f32[960]{0:T(1024)S(1)} %broadcast_multiply_fusion), kind=kOutput, calls=%fused_computation.68 | convolution fusion | flops 8076656640 | bytes 20225536 | tf_op jit(solution)/shard_map/dot_general | solution.py:34
  97.9 58.2 %all-gather.7.cloned.1.call-done = bf16[4096,1024]{0,1:T(8,128)(2,1)} async-done(((bf16[4096,64]{0,1:T(8,128)(2,1)}), bf16[4096,1024]{0,1:T(8,128)(2,1)}) %all-gather.7.cloned.1.call-update) | async-done | bytes 8388624 | tf_op jit(solution)/shard_map/all_gather | solution.py:41
  156.1 72.6 %all-gather.9.cloned.1.call-done = bf16[4096,1024]{0,1:T(8,128)(2,1)} async-done(((bf16[4096,64]{0,1:T(8,128)(2,1)}), bf16[4096,1024]{0,1:T(8,128)(2,1)}) %all-gather.9.cloned.1.call-update) | async-done | bytes 8388624 | tf_op jit(solution)/shard_map/all_gather | solution.py:47
  228.7 25.9 %convolution_convert_fusion = bf16[960,4096]{1,0:T(8,128)(2,1)} fusion(bf16[4096,1024]{0,1:T(8,128)(2,1)} %all-gather.9.cloned.1.call-done, f32[960,1024]{1,0:T(8,128)} %fusion.31, bf16[4096,1024]{0,1:T(8,128)(2,1)} %all-gather.7.cloned.1.call-done, bf16[960,4096]{1,0:T(8,128)(2,1)} %param.10, f32[4096]{0:T(1024)S(1)} %copy-done.4, f32[4096]{0:T(1024)S(1)} %copy-done.5, ...), kind=kOutput, calls=%fused_computation.13 | convolution fusion | flops 16139550720 | bytes 36478464 | tf_op jit(solution)/shard_map/dot_general | solution.py:45
  254.7 11.3 %convert_element_type.26 = f32[960,4096]{1,0:T(8,128)} convert(bf16[960,4096]{1,0:T(8,128)(2,1)} %param.10) | non-fusion elementwise | flops 3932160 | bytes 23592960 | tf_op jit(solution)/shard_map/convert_element_type | solution.py:32
  266.0 0.8 dynamic_slice.13
  266.7 37.6 %reduce-scatter.3.cloned.1.call-done = bf16[960,512]{1,0:T(8,128)(2,1)} async-done(((bf16[960,4096]{1,0:T(8,128)(2,1)}), bf16[960,512]{1,0:T(8,128)(2,1)}) %reduce-scatter.3.cloned.1.call-update) | async-done | bytes 983056 | tf_op jit(solution)/shard_map/reduce_scatter | solution.py:52
  304.3 2.2 add_convert_fusion.1
  306.5 1.5 reshape.67
  308.1 2.5 select_reduce_fusion.1
  310.6 2.4 convert_reduce_fusion.1
  313.1 14.6 %scatter_custom_fusion = s32[3840]{0:T(1024)S(1)} fusion(s32[3840]{0:T(1024)S(1)} %compare_select_fusion, s32[3840]{0:T(1024)S(1)} %iota.16, s32[]{:T(128)} %constant.104.clone.1), kind=kCustom, calls=%fused_computation.51 | custom fusion | bytes 15364 | tf_op jit(solution)/shard_map/scatter | solution.py:79
  327.7 86.2 %all-gather.11.cloned.1.call-done = bf16[3840,2048]{1,0:T(8,128)(2,1)} async-done(((bf16[240,2048]{1,0:T(8,128)(2,1)}), bf16[3840,2048]{1,0:T(8,128)(2,1)}) %all-gather.11.cloned.1.call-update) | async-done | bytes 15728656 | tf_op jit(solution)/shard_map/all_gather | solution.py:81
  413.9 37.0 %gather_fusion = bf16[3840,2048]{1,0:T(8,128)(2,1)} fusion(bf16[3840,2048]{1,0:T(8,128)(2,1)} %all-gather.11.cloned.1.call-done, s32[4096]{0:T(1024)S(1)} %pad_clamp_fusion), kind=kCustom, calls=%fused_computation | custom fusion | bytes 31472640 | tf_op jit(solution)/shard_map/jit(_take)/gather | solution.py:82
  450.9 9.9 %fusion.7 = bf16[3840,256]{1,0:T(8,128)(2,1)} fusion(bf16[2048,256]{1,0:T(8,128)(2,1)S(1)} %bitcast.13, bf16[3840,2048]{1,0:T(8,128)(2,1)} %gather_fusion, pred[3840]{0:T(1024)(128)(4,1)S(1)} %get-tuple-element.5, pred[3840]{0:T(1024)(128)(4,1)S(1)} %get-tuple-element.4), kind=kOutput, calls=%fused_computation.14 | convolution fusion | flops 4043243520 | bytes 18750976 | tf_op jit(solution)/shard_map/dot_general | solution.py:85
  460.8 0.6 dynamic_slice.14
  461.4 0.6 dynamic_slice.15
  462.1 31.9 %reduce-scatter.5.cloned.1.call-done = bf16[480,256]{1,0:T(8,128)(2,1)} async-done(((bf16[3840,256]{1,0:T(8,128)(2,1)}), bf16[480,256]{1,0:T(8,128)(2,1)}) %reduce-scatter.5.cloned.1.call-update) | async-done | bytes 245776 | tf_op jit(solution)/shard_map/reduce_scatter | solution.py:84
  494.0 1.7 all_to_all.14
  495.7 6.9 %all-to-all-start = ((bf16[16,30,256]{2,1,0:T(8,128)(2,1)}), bf16[16,30,256]{2,1,0:T(8,128)(2,1)S(1)}, u32[]{:S(2)}, u32[]{:S(2)}) async-start(bf16[16,30,256]{2,1,0:T(8,128)(2,1)} %all_to_all.14), calls=%async_computation.2 | async-start | bytes 524288 | tf_op jit(solution)/shard_map/all_to_all | solution.py:90
  502.6 1.3 fusion.27
  503.9 0.6 compare_select_fusion.1
  504.6 6.5 %all-to-all-done = bf16[16,30,256]{2,1,0:T(8,128)(2,1)S(1)} async-done(((bf16[16,30,256]{2,1,0:T(8,128)(2,1)}), bf16[16,30,256]{2,1,0:T(8,128)(2,1)S(1)}, u32[]{:S(2)}, u32[]{:S(2)}) %all-to-all-start) | async-done | bytes 245792 | tf_op jit(solution)/shard_map/all_to_all | solution.py:90
  511.4 4.4 gather_fusion.1
  515.7 5.3 select_select_fusion
  (32 shorter events, 0.7 us)
Async XLA Ops:
  7.2 443.7 %copy-start = (bf16[4,512,256]{2,1,0:T(8,128)(2,1)S(1)}, bf16[4,512,256]{2,1,0:T(8,128)(2,1)}, u32[]{:S(2)}) copy-start(bf16[4,512,256]{2,1,0:T(8,128)(2,1)} %param.17) | copy-start | bytes 3145732
  7.2 76.3 %all-gather.5.cloned.1.call-start = ((), (), s32[]{:S(2)}) async-start(), calls=%async_computation.3 | async-start | bytes 8912896 | tf_op jit(solution)/shard_map/all_gather | solution.py:36
  7.9 148.2 %all-gather.7.cloned.1.call-start = ((), (), s32[]{:S(2)}) async-start(), calls=%async_computation.4 | async-start | bytes 8912896 | tf_op jit(solution)/shard_map/all_gather | solution.py:41
  8.7 220.1 %all-gather.9.cloned.1.call-start = ((), (), s32[]{:S(2)}) async-start(), calls=%async_computation.5 | async-start | bytes 8912896 | tf_op jit(solution)/shard_map/all_gather | solution.py:47
  9.4 294.9 %reduce-scatter.3.cloned.1.call-start = ((), (), s32[]{:S(2)}) async-start(), calls=%async_computation.6 | async-start | bytes 8847360 | tf_op jit(solution)/shard_map/reduce_scatter | solution.py:52
  9.4 5.5 %copy-start.1 = (bf16[960,4096]{1,0:T(8,128)(2,1)S(1)}, bf16[960,4096]{1,0:T(8,128)(2,1)}, u32[]{:S(2)}) copy-start(bf16[960,4096]{1,0:T(8,128)(2,1)} %param.10) | copy-start | bytes 23592964
  9.5 74.1 %copy-start.4 = (f32[4096]{0:T(1024)S(1)}, f32[4096]{0:T(1024)}, u32[]{:S(2)}) copy-start(f32[4096]{0:T(1024)} %param.12) | copy-start | bytes 49156
  9.5 74.1 %copy-start.5 = (f32[4096]{0:T(1024)S(1)}, f32[4096]{0:T(1024)}, u32[]{:S(2)}) copy-start(f32[4096]{0:T(1024)} %param.11) | copy-start | bytes 49156
  254.6 159.3 %all-gather.11.cloned.1.call-start = ((), (), s32[]{:S(2)}) async-start(), calls=%async_computation.7 | async-start | bytes 16711680 | tf_op jit(solution)/shard_map/all_gather | solution.py:81
  254.7 53.4 %copy-start.3 = (s32[3840]{0:T(1024)S(1)}, s32[3840]{0:T(1024)}, u32[]{:S(2)}) copy-start(s32[3840]{0:T(1024)} %param.19) | copy-start | bytes 46084
  306.5 144.4 %copy-start.2 = (bf16[960,512]{1,0:T(8,128)(2,1)}, bf16[960,512]{1,0:T(8,128)(2,1)S(1)}, u32[]{:S(2)}) copy-start(bf16[960,512]{1,0:T(8,128)(2,1)S(1)} %add_convert_fusion.1) | copy-start | bytes 2949124
  308.0 186.0 %reduce-scatter.5.cloned.1.call-start = ((), (), s32[]{:S(2)}) async-start(), calls=%async_computation.8 | async-start | bytes 2211840 | tf_op jit(solution)/shard_map/reduce_scatter | solution.py:84
  495.7 15.4 %all-to-all-start = ((bf16[16,30,256]{2,1,0:T(8,128)(2,1)}), bf16[16,30,256]{2,1,0:T(8,128)(2,1)S(1)}, u32[]{:S(2)}, u32[]{:S(2)}) async-start(bf16[16,30,256]{2,1,0:T(8,128)(2,1)} %all_to_all.14), calls=%async_computation.2 | async-start | bytes 524288 | tf_op jit(solution)/shard_map/all_to_all | solution.py:90
Sparse Core Ops, SparseCore 0:
  10.2 73.3 all-gather.4
  85.7 70.4 all-gather.6
  158.3 70.4 all-gather.8
  254.7 49.5 reduce-scatter.2
  308.2 105.6 all-gather.10
  460.9 33.0 reduce-scatter.4
where the time goes:
time: 528 us
  waiting for transfers between devices  362 us (69%)
  local copies, waits for them, and re-layouts  62.5 us (12%)
  matrix products  50.1 us (9%)
  other arithmetic  32.3 us (6%)
  between operations  14.3 us (3%)
  starting transfers between devices  7.14 us (1%)
    all_gather x1, waiting for transfers between devices, shards(): every_row = lax.all_gather(merged, 'req', axis=0, tiled=True)  86.2 us
    all_gather x1, waiting for transfers between devices, shards(): lax.all_gather(down_weight, 'req', axis=1, tiled=True)  72.6 us
    all_gather x1, waiting for transfers between devices, shards(): lax.all_gather(gate_weight, 'req', axis=1, tiled=True)  66.4 us
    all_gather x1, waiting for transfers between devices, shards(): lax.all_gather(up_weight, 'req', axis=1, tiled=True)  58.2 us
    reduce_scatter x1, waiting for transfers between devices, shards(): lax.psum_scatter(partial_value.astype(jnp.bfloat16), 'mlp', scatter_dimen...  37.6 us
    gather x1, local copies, waits for them, and re-layouts, shards(): picked_rows = jnp.take(every_row, jnp.maximum(sources, 0), axis=0)  37 us
    reduce_scatter x1, waiting for transfers between devices, shards(): lax.psum_scatter(jnp.dot(picked_rows, weight_cols, preferred_element_type...  31.9 us
    dot_general x1, matrix products, shards(): lax.dot_general(hidden, lax.all_gather(down_weight, 'req', axis=1, tiled=...  25.9 us
  transfers between devices with their start and end apart: 7, of which 7 were waited for; matrix products, arithmetic and copies ran while one was open for 11% of the time, Pallas kernels for 0%

commit v1 on v0

--- a/solution.py
+++ b/solution.py
@@ -23,6 +23,14 @@
     text_rows,
     destination,
 ):
+
+    def lift_runs(message):
+        k_now = jnp.stack(jnp.split(message, lax.psum(1, axis_name="req"), 0))
+        side_arr = jnp.concatenate(
+            lax.all_to_all(k_now, axis_name="req", split_axis=0, concat_axis=0), axis=1
+        )
+        return side_arr
+
     req_count = lax.axis_size("req")
     mlp_count = lax.axis_size("mlp")
     req_index = lax.axis_index("req")
@@ -87,7 +95,7 @@
         scatter_dimension=0,
         tiled=True,
     )
-    arrived = lax.all_to_all(summed, "req", split_axis=0, concat_axis=1, tiled=True)
+    arrived = lift_runs(summed)
     bucket_here = req_index * mlp_count + mlp_index
     start_here = first_off[bucket_here]
     count_here = counts[bucket_here]

time: 528 us -> 549 us (1.040)
  local copies, waits for them, and re-layouts: 62.5 us -> 82.1 us
    unnamed x14 -> x29, local copies, waits for them, and re-layouts: 1.09 us -> 21.1 us
  transfers between devices with their start and end apart: 7 -> 7, of which waited for: 7 -> 7; matrix products, arithmetic and copies ran while one was open for 11% -> 10% of each run, Pallas kernels for 0% -> 0%
where the time goes in v1:
time: 549 us; the launch traced here: 547 us
  waiting for transfers between devices  362 us (66%)
  local copies, waits for them, and re-layouts  82.1 us (15%)
  matrix products  50.1 us (9%)
  other arithmetic  32.3 us (6%)
  between operations  14.3 us (3%)
  starting transfers between devices  7.14 us (1%)
    all_gather x1, waiting for transfers between devices, shards(): every_row = lax.all_gather(merged, 'req', axis=0, tiled=True)  86.2 us
    all_gather x1, waiting for transfers between devices, shards(): lax.all_gather(down_weight, 'req', axis=1, tiled=True)  72.6 us
    all_gather x1, waiting for transfers between devices, shards(): lax.all_gather(gate_weight, 'req', axis=1, tiled=True)  66.4 us
    all_gather x1, waiting for transfers between devices, shards(): lax.all_gather(up_weight, 'req', axis=1, tiled=True)  58.2 us
    reduce_scatter x1, waiting for transfers between devices, shards(): lax.psum_scatter(partial_value.astype(jnp.bfloat16), 'mlp', scatter_dimen...  37.6 us
    gather x1, local copies, waits for them, and re-layouts, shards(): picked_rows = jnp.take(every_row, jnp.maximum(sources, 0), axis=0)  37 us
    reduce_scatter x1, waiting for transfers between devices, shards(): lax.psum_scatter(jnp.dot(picked_rows, weight_cols, preferred_element_type...  31.9 us
    dot_general x1, matrix products, shards(): lax.dot_general(hidden, lax.all_gather(down_weight, 'req', axis=1, tiled=...  25.9 us
  transfers between devices with their start and end apart: 7, of which 7 were waited for; matrix products, arithmetic and copies ran while one was open for 10% of the time, Pallas kernels for 0%

profile of v1, /device:TPU:0, one launch (start us, length us, event | category | flops | bytes accessed | tf_op | source)
XLA Modules:
  0.0 547.5 jit_solution(13415283467542613330)
XLA Ops:
  9.5 4.5 convert_reduce_fusion
  14.9 2.2 multiply_reduce_fusion
  17.1 66.4 %all-gather.5.cloned.1.call-done = bf16[4096,1024]{0,1:T(8,128)(2,1)} async-done(((bf16[4096,64]{0,1:T(8,128)(2,1)}), bf16[4096,1024]{0,1:T(8,128)(2,1)}) %all-gather.5.cloned.1.call-update) | async-done | bytes 8388624 | tf_op jit(solution)/shard_map/all_gather | solution.py:44
  83.5 14.4 %fusion.31 = f32[960,1024]{1,0:T(8,128)} fusion(bf16[4096,1024]{0,1:T(8,128)(2,1)} %all-gather.5.cloned.1.call-done, bf16[960,4096]{1,0:T(8,128)(2,1)} %param.10, f32[4096]{0:T(1024)S(1)} %copy-done.4, f32[4096]{0:T(1024)S(1)} %copy-done.5, f32[960]{0:T(1024)S(1)} %add_rsqrt_fusion, f32[960]{0:T(1024)S(1)} %broadcast_multiply_fusion), kind=kOutput, calls=%fused_computation.100 | convolution fusion | flops 8076656640 | bytes 20225536 | tf_op jit(solution)/shard_map/dot_general | solution.py:42
  97.9 58.2 %all-gather.7.cloned.1.call-done = bf16[4096,1024]{0,1:T(8,128)(2,1)} async-done(((bf16[4096,64]{0,1:T(8,128)(2,1)}), bf16[4096,1024]{0,1:T(8,128)(2,1)}) %all-gather.7.cloned.1.call-update) | async-done | bytes 8388624 | tf_op jit(solution)/shard_map/all_gather | solution.py:49
  156.1 72.6 %all-gather.9.cloned.1.call-done = bf16[4096,1024]{0,1:T(8,128)(2,1)} async-done(((bf16[4096,64]{0,1:T(8,128)(2,1)}), bf16[4096,1024]{0,1:T(8,128)(2,1)}) %all-gather.9.cloned.1.call-update) | async-done | bytes 8388624 | tf_op jit(solution)/shard_map/all_gather | solution.py:55
  228.7 25.9 %convolution_convert_fusion = bf16[960,4096]{1,0:T(8,128)(2,1)} fusion(bf16[4096,1024]{0,1:T(8,128)(2,1)} %all-gather.9.cloned.1.call-done, f32[960,1024]{1,0:T(8,128)} %fusion.31, bf16[4096,1024]{0,1:T(8,128)(2,1)} %all-gather.7.cloned.1.call-done, bf16[960,4096]{1,0:T(8,128)(2,1)} %param.10, f32[4096]{0:T(1024)S(1)} %copy-done.4, f32[4096]{0:T(1024)S(1)} %copy-done.5, ...), kind=kOutput, calls=%fused_computation.13 | convolution fusion | flops 16139550720 | bytes 36478464 | tf_op jit(solution)/shard_map/dot_general | solution.py:53
  254.7 11.3 %convert_element_type.26 = f32[960,4096]{1,0:T(8,128)} convert(bf16[960,4096]{1,0:T(8,128)(2,1)} %param.10) | non-fusion elementwise | flops 3932160 | bytes 23592960 | tf_op jit(solution)/shard_map/convert_element_type | solution.py:40
  266.7 37.6 %reduce-scatter.3.cloned.1.call-done = bf16[960,512]{1,0:T(8,128)(2,1)} async-done(((bf16[960,4096]{1,0:T(8,128)(2,1)}), bf16[960,512]{1,0:T(8,128)(2,1)}) %reduce-scatter.3.cloned.1.call-update) | async-done | bytes 983056 | tf_op jit(solution)/shard_map/reduce_scatter | solution.py:60
  304.3 2.2 add_convert_fusion.1
  306.5 1.5 reshape.70
  308.1 2.5 select_reduce_fusion.1
  310.6 2.4 convert_reduce_fusion.1
  313.1 14.6 %scatter_custom_fusion = s32[3840]{0:T(1024)S(1)} fusion(s32[3840]{0:T(1024)S(1)} %compare_select_fusion, s32[3840]{0:T(1024)S(1)} %iota.16, s32[]{:T(128)} %constant.104.clone.1), kind=kCustom, calls=%fused_computation.83 | custom fusion | bytes 15364 | tf_op jit(solution)/shard_map/scatter | solution.py:87
  327.7 86.2 %all-gather.11.cloned.1.call-done = bf16[3840,2048]{1,0:T(8,128)(2,1)} async-done(((bf16[240,2048]{1,0:T(8,128)(2,1)}), bf16[3840,2048]{1,0:T(8,128)(2,1)}) %all-gather.11.cloned.1.call-update) | async-done | bytes 15728656 | tf_op jit(solution)/shard_map/all_gather | solution.py:89
  413.9 37.0 %gather_fusion = bf16[3840,2048]{1,0:T(8,128)(2,1)} fusion(bf16[3840,2048]{1,0:T(8,128)(2,1)} %all-gather.11.cloned.1.call-done, s32[4096]{0:T(1024)S(1)} %pad_clamp_fusion), kind=kCustom, calls=%fused_computation | custom fusion | bytes 31472640 | tf_op jit(solution)/shard_map/jit(_take)/gather | solution.py:90
  450.9 9.9 %fusion.7 = bf16[3840,256]{1,0:T(8,128)(2,1)} fusion(bf16[2048,256]{1,0:T(8,128)(2,1)S(1)} %bitcast.77, bf16[3840,2048]{1,0:T(8,128)(2,1)} %gather_fusion, pred[3840]{0:T(1024)(128)(4,1)S(1)} %get-tuple-element.5, pred[3840]{0:T(1024)(128)(4,1)S(1)} %get-tuple-element.4), kind=kOutput, calls=%fused_computation.14 | convolution fusion | flops 4043243520 | bytes 18750976 | tf_op jit(solution)/shard_map/dot_general | solution.py:93
  462.1 31.9 %reduce-scatter.5.cloned.1.call-done = bf16[480,256]{1,0:T(8,128)(2,1)} async-done(((bf16[3840,256]{1,0:T(8,128)(2,1)}), bf16[480,256]{1,0:T(8,128)(2,1)}) %reduce-scatter.5.cloned.1.call-update) | async-done | bytes 245776 | tf_op jit(solution)/shard_map/reduce_scatter | solution.py:92
  495.3 1.3 constant_dynamic-update-slice_fusion.14
  496.7 1.3 constant_dynamic-update-slice_fusion.13
  498.0 1.3 constant_dynamic-update-slice_fusion.12
  500.7 1.3 constant_dynamic-update-slice_fusion.10
  502.0 1.3 constant_dynamic-update-slice_fusion.9
  503.3 1.3 constant_dynamic-update-slice_fusion.8
  506.0 1.3 constant_dynamic-update-slice_fusion.6
  507.3 1.3 constant_dynamic-update-slice_fusion.5
  508.7 1.3 constant_dynamic-update-slice_fusion.4
  511.3 1.3 constant_dynamic-update-slice_fusion.2
  515.3 6.9 %all-to-all-start = ((bf16[16,30,256]{2,1,0:T(8,128)(2,1)}), bf16[16,30,256]{2,1,0:T(8,128)(2,1)S(1)}, u32[]{:S(2)}, u32[]{:S(2)}) async-start(bf16[16,30,256]{2,1,0:T(8,128)(2,1)} %constant_dynamic-update-slice_fusion), calls=%async_computation.2 | async-start | bytes 524288 | tf_op jit(solution)/shard_map/all_to_all | solution.py:30
  524.2 6.5 %all-to-all-done = bf16[16,30,256]{2,1,0:T(8,128)(2,1)S(1)} async-done(((bf16[16,30,256]{2,1,0:T(8,128)(2,1)}), bf16[16,30,256]{2,1,0:T(8,128)(2,1)S(1)}, u32[]{:S(2)}, u32[]{:S(2)}) %all-to-all-start) | async-done | bytes 245792 | tf_op jit(solution)/shard_map/all_to_all | solution.py:30
  531.0 4.4 gather_fusion.1
  535.4 5.3 select_select_fusion
  (47 shorter events, 15.6 us)
Async XLA Ops:
  7.2 443.7 %copy-start = (bf16[4,512,256]{2,1,0:T(8,128)(2,1)S(1)}, bf16[4,512,256]{2,1,0:T(8,128)(2,1)}, u32[]{:S(2)}) copy-start(bf16[4,512,256]{2,1,0:T(8,128)(2,1)} %param.17) | copy-start | bytes 3145732
  7.2 76.3 %all-gather.5.cloned.1.call-start = ((), (), s32[]{:S(2)}) async-start(), calls=%async_computation.3 | async-start | bytes 8912896 | tf_op jit(solution)/shard_map/all_gather | solution.py:44
  7.9 148.2 %all-gather.7.cloned.1.call-start = ((), (), s32[]{:S(2)}) async-start(), calls=%async_computation.4 | async-start | bytes 8912896 | tf_op jit(solution)/shard_map/all_gather | solution.py:49
  8.7 220.1 %all-gather.9.cloned.1.call-start = ((), (), s32[]{:S(2)}) async-start(), calls=%async_computation.5 | async-start | bytes 8912896 | tf_op jit(solution)/shard_map/all_gather | solution.py:55
  9.4 294.9 %reduce-scatter.3.cloned.1.call-start = ((), (), s32[]{:S(2)}) async-start(), calls=%async_computation.6 | async-start | bytes 8847360 | tf_op jit(solution)/shard_map/reduce_scatter | solution.py:60
  9.4 5.5 copy-start.1
  9.5 74.1 %copy-start.4 = (f32[4096]{0:T(1024)S(1)}, f32[4096]{0:T(1024)}, u32[]{:S(2)}) copy-start(f32[4096]{0:T(1024)} %param.12) | copy-start | bytes 49156
  9.5 74.1 %copy-start.5 = (f32[4096]{0:T(1024)S(1)}, f32[4096]{0:T(1024)}, u32[]{:S(2)}) copy-start(f32[4096]{0:T(1024)} %param.11) | copy-start | bytes 49156
  254.6 159.3 %all-gather.11.cloned.1.call-start = ((), (), s32[]{:S(2)}) async-start(), calls=%async_computation.7 | async-start | bytes 16711680 | tf_op jit(solution)/shard_map/all_gather | solution.py:89
  254.7 53.4 %copy-start.3 = (s32[3840]{0:T(1024)S(1)}, s32[3840]{0:T(1024)}, u32[]{:S(2)}) copy-start(s32[3840]{0:T(1024)} %param.19) | copy-start | bytes 46084
  306.5 144.4 %copy-start.2 = (bf16[960,512]{1,0:T(8,128)(2,1)}, bf16[960,512]{1,0:T(8,128)(2,1)S(1)}, u32[]{:S(2)}) copy-start(bf16[960,512]{1,0:T(8,128)(2,1)S(1)} %add_convert_fusion.1) | copy-start | bytes 2949124
  308.0 186.0 %reduce-scatter.5.cloned.1.call-start = ((), (), s32[]{:S(2)}) async-start(), calls=%async_computation.8 | async-start | bytes 2211840 | tf_op jit(solution)/shard_map/reduce_scatter | solution.py:92
  515.3 15.4 %all-to-all-start = ((bf16[16,30,256]{2,1,0:T(8,128)(2,1)}), bf16[16,30,256]{2,1,0:T(8,128)(2,1)S(1)}, u32[]{:S(2)}, u32[]{:S(2)}) async-start(bf16[16,30,256]{2,1,0:T(8,128)(2,1)} %constant_dynamic-update-slice_fusion), calls=%async_computation.2 | async-start | bytes 524288 | tf_op jit(solution)/shard_map/all_to_all | solution.py:30
Sparse Core Ops, SparseCore 0:
  10.2 73.3 all-gather.4
  85.7 70.4 all-gather.6
  158.3 70.4 all-gather.8
  254.7 49.5 reduce-scatter.2
  308.2 105.6 all-gather.10
  460.9 33.0 reduce-scatter.4
